TPU v7x, 32 devices: a whole 2x2x4 slice. The times are simulated.
32 devices in a mesh: groups: 2 (over y), blk: 4 (over z), oct: 2 (over x), sub: 2 (over core).
Axes of the slice: x: 2, y: 2, z: 4, core: 2. Of those that a mesh axis runs over, the one named last changes fastest.
Arguments:
- positions: float32 [3, 65536], P(None, ('groups', 'blk', 'oct', 'sub')), parts along dimension 1, may hold values from 0 to 320
- polarizability: float32 [65536], P(('groups', 'blk', 'oct', 'sub')), parts along dimension 0, may hold values from 0.5 to 1.5
- permanent_field: float32 [3, 65536], P(None, ('groups', 'blk', 'oct', 'sub')), parts along dimension 1, may hold values from -40 to 40
- group_id: int32 [65536], P(('groups', 'blk', 'oct', 'sub')), parts along dimension 0, may hold values from 0 to 10921, never falling along the last dimension, each value on 1 to 6 neighbouring positions
- pair_mask: int32 [512, 9], P(('groups', 'blk', 'oct', 'sub')), parts along dimension 0, may hold values from 0 to 1, as said below
Outputs:
- dipoles: float32 [3, 65536], P(None, ('groups', 'blk', 'oct', 'sub')), parts along dimension 1
- residual: float32 [3, 65536], P(None, ('groups', 'blk', 'oct', 'sub')), parts along dimension 1
There are 2 independent parts, one for each index of `groups`. A program takes and returns all parts, laid end to end along the dimension named above; each array names one. Nothing has to cross between parts.
Inputs may be any that keep to these rules, and one draw needn't show every extreme that they name: `group_id`: never falls from one atom to the next; each value names 1 to 6 consecutive atoms. pair_mask[b, 4] = 1, and pair_mask[b, 4 + o] = pair_mask[(b + o) mod 256, 4 - o].
All inputs are finite; a program needn't handle non-finite values.
Results may differ from a plain program's by a relative error of at most 0.0003.
Values sent between devices are 32-bit elements; how exact they have to be, the bound alone decides.
No kernel may reach another device: no remote copies, remote signals or barrier semaphores. Data moves between devices by JAX's collectives and lax.ppermute only.
A program may use at most 64 MiB of HBM per device.

v0:
```python
import math
import jax
import jax.numpy as jnp
import numpy as np
from jax import lax
from jax.sharding import PartitionSpec as P

BOXES_DEV = 2
BLOCK = 128
ORDER = 5
NODE_PAD = 128
ITERS = 2
side_length = 32.0
layer_gap = 2.5
thole_damp = 0.39
highest = lax.Precision.HIGHEST


def padded(cells, sides, width):
    for axis, dim in sides:
        count = lax.axis_size(axis)
        head = lax.slice_in_dim(cells, 0, width, axis=dim)
        tail = lax.slice_in_dim(cells, cells.shape[dim] - width, cells.shape[dim], axis=dim)
        cells = jnp.concatenate(
            [
                lax.ppermute(tail, axis, [(i, (i + 1) % count) for i in range(count)]),
                cells,
                lax.ppermute(head, axis, [((i + 1) % count, i) for i in range(count)]),
            ],
            axis=dim,
        )
    return cells


def wrap_image(delta, period):
    return delta - period * jnp.floor(delta / period + 0.5)


def split_size(total, limit):
    best = 1
    for factor in range(1, min(total, limit) + 1):
        if total % factor == 0:
            best = factor
    return best


def near_tiles(target, source, moments, keep_tile, length_z):
    delta_x = wrap_image(target[0][:, :, None] - source[0][:, None, :], side_length)
    delta_y = wrap_image(target[1][:, :, None] - source[1][:, None, :], side_length)
    delta_z = wrap_image(target[2][:, :, None] - source[2][:, None, :], length_z)
    keep = (keep_tile[:, None, None] > 0.5) & (target[4][:, :, None] != source[4][:, None, :])
    dist_sq = jnp.where(keep, delta_x * delta_x + delta_y * delta_y + delta_z * delta_z, 1.0)
    inv_three = lax.rsqrt(dist_sq) / dist_sq
    scaled = (
        thole_damp
        * dist_sq
        * jnp.sqrt(dist_sq)
        * lax.rsqrt(target[3][:, :, None] * source[3][:, None, :])
    )
    lam_three = -jnp.expm1(-scaled)
    lam_five = lam_three - scaled * jnp.exp(-scaled)
    coef_five = jnp.where(keep, 3.0 * lam_five * inv_three / dist_sq, 0.0)
    coef_three = jnp.where(keep, lam_three * inv_three, 0.0)
    along = (
        delta_x * moments[0][:, None, :]
        + delta_y * moments[1][:, None, :]
        + delta_z * moments[2][:, None, :]
    )
    weighted = coef_five * along
    field_x = jnp.sum(weighted * delta_x - coef_three * moments[0][:, None, :], axis=2)
    field_y = jnp.sum(weighted * delta_y - coef_three * moments[1][:, None, :], axis=2)
    field_z = jnp.sum(weighted * delta_z - coef_three * moments[2][:, None, :], axis=2)
    return jnp.stack([field_x, field_y, field_z])


def near_total(static_ext, dipole_ext, mask_rows, length_z, atom_count):
    reach = (mask_rows.shape[1] - 1) // 2
    width = reach * BLOCK
    blocks = atom_count // BLOCK
    target = static_ext[:, width : width + atom_count].reshape(5, blocks, BLOCK)
    total = jnp.zeros((3, blocks, BLOCK), static_ext.dtype)
    for offset in range(-reach, reach + 1):
        begin = (reach + offset) * BLOCK
        source = static_ext[:, begin : begin + atom_count].reshape(5, blocks, BLOCK)
        moments = dipole_ext[:, begin : begin + atom_count].reshape(3, blocks, BLOCK)
        keep_tile = mask_rows[:, reach + offset].astype(static_ext.dtype)
        total = total + near_tiles(target, source, moments, keep_tile, length_z)
    return total.reshape(3, atom_count)


def node_tables():
    count = ORDER
    roots = np.cos((2.0 * np.arange(count) + 1.0) * np.pi / (2.0 * count))
    degree = np.arange(count)
    coeff = (
        2.0 / count * np.cos(np.outer(2.0 * np.arange(count) + 1.0, degree) * np.pi / (2.0 * count))
    )
    coeff = np.where(degree[None, :] == 0, 1.0 / count, coeff)
    index = np.arange(NODE_PAD)
    live = index < count**3
    safe = np.where(live, index, 0)
    first = safe // (count * count)
    second = safe // count % count
    third = safe % count
    levels = np.arange(count)[None, :]
    pick_a = (first[:, None] == levels) * live[:, None] * 1.0
    pick_b = (second[:, None] == levels) * 1.0
    pick_c = (third[:, None] == levels) * 1.0
    node_x = 16.0 * (1.0 + roots[first])
    node_y = 16.0 * (1.0 + roots[second])
    node_t = roots[third]
    tables = [coeff, pick_a, pick_b, pick_c, node_x, node_y, node_t]
    return [jnp.asarray(item, jnp.float32) for item in tables]


def interpolation(coords, box_ids, box_height):
    coeff, pick_a, pick_b, pick_c, node_x, node_y, node_t = node_tables()
    scaled_x = coords[0] / 16.0 - 1.0
    scaled_y = coords[1] / 16.0 - 1.0
    scaled_z = (
        2.0 * (coords[2] - box_ids.astype(coords.dtype)[:, None] * box_height) / box_height - 1.0
    )

    def basis(values, picks):
        terms = [jnp.ones_like(values), values]
        for degree in range(2, ORDER):
            terms.append(2.0 * values * terms[-1] - terms[-2])
        stacked = jnp.stack(terms[:ORDER])
        smooth = jnp.einsum("kn,nba->kba", coeff, stacked, precision=highest)
        return jnp.einsum("pk,kba->pba", picks, smooth, precision=highest)

    return basis(scaled_x, pick_a) * basis(scaled_y, pick_b) * basis(scaled_z, pick_c)


def far_block(target_ids, source_ids, weights, slabs, box_height, length_z):
    coeff, pick_a, pick_b, pick_c, node_x, node_y, node_t = node_tables()
    height_t = (
        target_ids.astype(weights.dtype)[:, None] * box_height
        + 0.5 * box_height * (1.0 + node_t)[None, :]
    )
    height_s = (
        source_ids.astype(weights.dtype)[:, None] * box_height
        + 0.5 * box_height * (1.0 + node_t)[None, :]
    )
    delta_x = wrap_image(node_x[:, None] - node_x[None, :], side_length)[None, :, None, :]
    delta_y = wrap_image(node_y[:, None] - node_y[None, :], side_length)[None, :, None, :]
    delta_z = wrap_image(height_t[:, :, None, None] - height_s[None, None, :, :], length_z)
    apart = jnp.abs(target_ids[:, None] // BOXES_DEV - source_ids[None, :] // BOXES_DEV)
    apart = jnp.minimum(apart, slabs - apart)
    keep = (apart >= 1)[:, None, :, None]
    dist_sq = jnp.where(
        keep,
        delta_x * delta_x + delta_y * delta_y + delta_z * delta_z + box_height * box_height,
        1.0,
    )
    inv_three = lax.rsqrt(dist_sq) / dist_sq
    coef_five = jnp.where(keep, 3.0 * inv_three / dist_sq, 0.0)
    coef_three = jnp.where(keep, inv_three, 0.0)
    weight_x = weights[:, 0, :][None, None]
    weight_y = weights[:, 1, :][None, None]
    weight_z = weights[:, 2, :][None, None]
    weighted = coef_five * (delta_x * weight_x + delta_y * weight_y + delta_z * weight_z)
    field_x = jnp.sum(weighted * delta_x - coef_three * weight_x, axis=(2, 3))
    field_y = jnp.sum(weighted * delta_y - coef_three * weight_y, axis=(2, 3))
    field_z = jnp.sum(weighted * delta_z - coef_three * weight_z, axis=(2, 3))
    return jnp.stack([field_x, field_y, field_z], axis=1)


def on_device(positions, polarizability, permanent_field, group_id, pair_mask):
    slabs = lax.axis_size(("blk", "oct", "sub"))
    member = lax.axis_index(("blk", "oct", "sub"))
    atom_count = positions.shape[1]
    length_z = layer_gap * atom_count * slabs / 256.0
    box_height = length_z / (BOXES_DEV * slabs)
    per_box = atom_count // BOXES_DEV
    width = (pair_mask.shape[1] - 1) // 2 * BLOCK
    group_limit = max(1, 32 // BOXES_DEV)
    static = jnp.concatenate(
        [positions, polarizability[None, :], group_id.astype(jnp.float32)[None, :]], axis=0
    )
    static_ext = padded(static, ((("blk", "oct", "sub"), 1),), width)
    own_boxes = member * BOXES_DEV + jnp.arange(BOXES_DEV, dtype=jnp.int32)
    interp = interpolation(positions.reshape(3, BOXES_DEV, per_box), own_boxes, box_height)
    surface = 4.0 * math.pi / 3.0 / (side_length * side_length * length_z)

    def induced(dipoles, total):
        dipole_ext = padded(dipoles, ((("blk", "oct", "sub"), 1),), width)
        near = near_total(static_ext, dipole_ext, pair_mask, length_z, atom_count)
        weights = jnp.einsum(
            "pba,cba->bcp", interp, dipoles.reshape(3, BOXES_DEV, per_box), precision=highest
        )
        piece = lax.all_gather(weights, ("blk", "oct", "sub"), axis=0, tiled=True)
        start = jnp.int32(0)
        count = piece.shape[0]
        size = split_size(count, group_limit)
        grouped = piece.reshape(count // size, size, 3, piece.shape[2])

        def visit(acc, item):
            index, bundle = item
            sources = start + index * size + jnp.arange(size, dtype=jnp.int32)
            return (acc + far_block(own_boxes, sources, bundle, slabs, box_height, length_z), None)

        result, unused = lax.scan(
            visit, jnp.zeros_like(weights), (jnp.arange(count // size, dtype=jnp.int32), grouped)
        )
        far = jnp.einsum("pba,bcp->cba", interp, result, precision=highest).reshape(3, atom_count)
        return near + far - surface * total[:, None]

    def moment(values):
        return lax.psum(jnp.sum(values, axis=1), ("blk", "oct", "sub"))

    def squares(resid, scaled):
        return lax.psum(jnp.sum(resid * scaled), ("blk", "oct", "sub"))

    dipoles = polarizability[None, :] * permanent_field
    residual = induced(dipoles, moment(dipoles))
    precond = polarizability[None, :] * residual
    direction = precond
    norm_now = squares(residual, precond)
    for step in range(ITERS):
        image = direction / polarizability[None, :] - induced(direction, moment(direction))
        rate = norm_now / lax.psum(jnp.sum(direction * image), ("blk", "oct", "sub"))
        dipoles = dipoles + rate * direction
        residual = residual - rate * image
        if step + 1 < ITERS:
            precond = polarizability[None, :] * residual
            norm_next = squares(residual, precond)
            direction = precond + norm_next / norm_now * direction
            norm_now = norm_next
    return (dipoles, residual)


def solution(mesh):
    return jax.shard_map(
        on_device,
        mesh=mesh,
        in_specs=(
            P(None, ("groups", "blk", "oct", "sub")),
            P(("groups", "blk", "oct", "sub")),
            P(None, ("groups", "blk", "oct", "sub")),
            P(("groups", "blk", "oct", "sub")),
            P(("groups", "blk", "oct", "sub"), None),
        ),
        out_specs=(
            P(None, ("groups", "blk", "oct", "sub")),
            P(None, ("groups", "blk", "oct", "sub")),
        ),
        check_vma=False,
    )
```

profile of v0, /device:TPU:0, one launch (start us, length us, event | category | flops | bytes accessed | tf_op | source)
XLA Modules:
  0.0 428.3 jit_solution(15247812564218952183)
XLA Ops:
  0.7 0.7 convert_bitcast_fusion
  1.4 0.8 pad_maximum_fusion.3
  2.6 5.0 %collective-permute-start.2 = (f32[5,512]{1,0:T(8,128)S(1)}, f32[5,512]{1,0:T(8,128)S(1)}, u32[]{:S(2)}, u32[]{:S(2)}) collective-permute-start(f32[5,512]{1,0:T(8,128)S(1)} %get-tuple-element.990), channel_id=1, source_target_pairs={{1,0},{2,1},{3,2},{4,3},{5,4},{6,5},{7,6},{8,7},{9,8},{10,9},{11,1... | collective-permute-start | bytes 30728 | tf_op jit(solution)/shard_map/ppermute | solution.py:28
  7.7 0.9 fusion.771
  8.6 4.4 %collective-permute-start.3 = (f32[3,512]{1,0:T(4,128)S(1)}, f32[3,512]{1,0:T(4,128)S(1)}, u32[]{:S(2)}, u32[]{:S(2)}) collective-permute-start(f32[3,512]{1,0:T(4,128)S(1)} %get-tuple-element.1086), channel_id=1, source_target_pairs={{1,0},{2,1},{3,2},{4,3},{5,4},{6,5},{7,6},{8,7},{9,8},{10,9},{11,1... | collective-permute-start | bytes 18440 | tf_op jit(solution)/shard_map/ppermute | solution.py:28
  13.1 0.9 fusion.777
  14.0 29.5 %psum.49 = f32[3]{0:T(128)S(1)} all-reduce(f32[3]{0:T(128)S(1)} %get-tuple-element.927), channel_id=1, replica_groups=mesh['groups'=2,'blk'=4,'oct'=2,'sub'=2] {'blk','oct','sub'}, use_global_device_ids=true, to_apply=%region_33.34 | all-reduce | flops 3 | bytes 24 | tf_op jit(solution)/shard_map/psum | solution.py:210
  43.8 0.9 fusion.780
  44.7 0.9 fusion.778
  45.9 1.8 fusion.779
  47.7 1.8 convolution_multiply_fusion.1
  49.6 1.8 fusion.90
  52.0 17.8 %all_gather.9 = f32[32,3,128]{2,1,0:T(4,128)S(1)} all-gather(f32[2,3,128]{2,1,0:T(4,128)S(1)} %fusion.782), channel_id=1, replica_groups=mesh['groups'=2,'blk'=4,'oct'=2,'sub'=2] {'blk','oct','sub'}, dimensions={0}, use_global_device_ids=true | all-gather | bytes 52224 | tf_op jit(solution)/shard_map/all_gather | solution.py:192
  69.9 13.5 %while.51 = (s32[]{:T(128)}, f32[2,3,128]{2,0,1:T(2,128)S(1)}, s32[2]{0:T(128)S(1)}, f32[2,16,3,128]{3,1,2,0:T(8,128)S(1)}, s32[]{:T(128)}, /*index=5*/s32[]{:T(...) while((s32[]{:T(128)}, f32[2,3,128]{2,0,1:T(2,128)S(1)}, ...), condition=%wide.region_31.32_spmd.clone.clone.clone.clone, body=%wide.region_27.31_spmd.sunk.clone.clone.clone.clone.sunk | while | flops 16765948 | bytes 2795035 | solution.py:203
  69.9 0.7 dynamic_slice.84
  71.8 4.8 %subtract_reduce_fusion.9 = (f32[2,128]{1,0:T(2,128)S(1)}, f32[2,128]{1,0:T(2,128)S(1)}, f32[2,128]{1,0:T(2,128)S(1)}) fusion(f32[16,128]{1,0:T(8,128)S(1)} %get-tuple-element.1216, f32[128,128]{1,0:T(8,128)S(1)} %get-tuple-element.1217, pred[2,16]{1,0:T(4,128)(4,1)S(1)} %fusion.814, f32[16,128]{1,0:T(8,128)S(1)} %broadcast_add_fusion.12, ...), kind=kLoop, calls=%fused_computation.28.clone.1 | loop fusion | flops 15727872 | bytes 1282080 | tf_op jit(solution)/shard_map/while/body/eval_jaxpr/reduce_sum | solution.py:163
  76.7 0.7 dynamic_slice.84
  78.5 4.8 %subtract_reduce_fusion.9 = (f32[2,128]{1,0:T(2,128)S(1)}, f32[2,128]{1,0:T(2,128)S(1)}, f32[2,128]{1,0:T(2,128)S(1)}) fusion(f32[16,128]{1,0:T(8,128)S(1)} %get-tuple-element.1216, f32[128,128]{1,0:T(8,128)S(1)} %get-tuple-element.1217, pred[2,16]{1,0:T(4,128)(4,1)S(1)} %fusion.814, f32[16,128]{1,0:T(8,128)S(1)} %broadcast_add_fusion.12, ...), kind=kLoop, calls=%fused_computation.28.clone.1 | loop fusion | flops 15727872 | bytes 1282080 | tf_op jit(solution)/shard_map/while/body/eval_jaxpr/reduce_sum | solution.py:163
  84.2 4.0 fusion.558
  88.2 4.0 fusion.585
  92.2 4.0 fusion.567
  96.2 4.0 fusion.576
  100.2 4.0 fusion.603
  104.2 4.0 fusion.621
  108.2 4.0 fusion.612
  112.2 7.3 %fusion.630 = (f32[16,128]{1,0:T(8,128)S(1)}, f32[16,128]{1,0:T(8,128)S(1)}, f32[16,128]{1,0:T(8,128)S(1)}, f32[16,128]{1,0:T(8,128)S(1)}, f32[16,128]{1,0:T(8,128)S(1)}, /*index=5*/f32[16,128]{1,0:T(8,128)S(1)}) fusion(f32[16,128]{1,0:T(8,128)S(1)} %bitcast.840, f32[16,128]{1,0:T(8,128)S(1)} %bitcast.735, f32[16,128]{1,0:T(8,128)S(1)} %bitcast.931, ...), kind=kLoop, calls=%fused_computation.815 | loop fusion | flops 30920704 | bytes 180256 | tf_op jit(solution)/shard_map/reduce_sum | solution.py:70
  119.5 1.1 multiply_reduce_fusion.2
  120.7 31.6 %psum.51 = f32[3]{0:T(128)S(1)} all-reduce(f32[3]{0:T(128)S(1)} %get-tuple-element.923), channel_id=1, replica_groups=mesh['groups'=2,'blk'=4,'oct'=2,'sub'=2] {'blk','oct','sub'}, use_global_device_ids=true, to_apply=%region_69.70 | all-reduce | flops 3 | bytes 24 | tf_op jit(solution)/shard_map/psum | solution.py:210
  152.3 0.6 fusion.684
  153.2 4.4 %collective-permute-start.5 = (f32[3,512]{1,0:T(4,128)S(1)}, f32[3,512]{1,0:T(4,128)S(1)}, u32[]{:S(2)}, u32[]{:S(2)}) collective-permute-start(f32[3,512]{1,0:T(4,128)S(1)} %get-tuple-element.1078), channel_id=1, source_target_pairs={{1,0},{2,1},{3,2},{4,3},{5,4},{6,5},{7,6},{8,7},{9,8},{10,9},{11,1... | collective-permute-start | bytes 18440 | tf_op jit(solution)/shard_map/ppermute | solution.py:28
  157.6 17.3 %all_gather.10 = f32[32,3,128]{2,1,0:T(4,128)S(1)} all-gather(f32[2,3,128]{2,1,0:T(4,128)S(1)} %fusion.684), channel_id=1, replica_groups=mesh['groups'=2,'blk'=4,'oct'=2,'sub'=2] {'blk','oct','sub'}, dimensions={0}, use_global_device_ids=true | all-gather | bytes 52224 | tf_op jit(solution)/shard_map/all_gather | solution.py:192
  174.9 13.0 %while.52 = (s32[]{:T(128)}, f32[2,3,128]{2,0,1:T(2,128)S(1)}, s32[2]{0:T(128)S(1)}, f32[2,16,3,128]{3,1,2,0:T(8,128)S(1)}, s32[]{:T(128)}, /*index=5*/s32[]{:T(...) while((s32[]{:T(128)}, f32[2,3,128]{2,0,1:T(2,128)S(1)}, ...), condition=%wide.region_67.68_spmd.clone.clone.clone.clone, body=%wide.region_63.67_spmd.sunk.clone.clone.clone.clone.sunk | while | flops 16765948 | bytes 2795035 | solution.py:203
  176.6 4.8 %subtract_reduce_fusion.10 = (f32[2,128]{1,0:T(2,128)S(1)}, f32[2,128]{1,0:T(2,128)S(1)}, f32[2,128]{1,0:T(2,128)S(1)}) fusion(f32[16,128]{1,0:T(8,128)S(1)} %get-tuple-element.1230, f32[128,128]{1,0:T(8,128)S(1)} %get-tuple-element.1231, pred[2,16]{1,0:T(4,128)(4,1)S(1)} %fusion.817, f32[16,128]{1,0:T(8,128)S(1)} %broadcast_add_fusion.14, ...), kind=kLoop, calls=%fused_computation.82.clone.1 | loop fusion | flops 15727872 | bytes 1282080 | tf_op jit(solution)/shard_map/while/body/eval_jaxpr/reduce_sum | solution.py:163
  183.1 4.8 %subtract_reduce_fusion.10 = (f32[2,128]{1,0:T(2,128)S(1)}, f32[2,128]{1,0:T(2,128)S(1)}, f32[2,128]{1,0:T(2,128)S(1)}) fusion(f32[16,128]{1,0:T(8,128)S(1)} %get-tuple-element.1230, f32[128,128]{1,0:T(8,128)S(1)} %get-tuple-element.1231, pred[2,16]{1,0:T(4,128)(4,1)S(1)} %fusion.817, f32[16,128]{1,0:T(8,128)S(1)} %broadcast_add_fusion.14, ...), kind=kLoop, calls=%fused_computation.82.clone.1 | loop fusion | flops 15727872 | bytes 1282080 | tf_op jit(solution)/shard_map/while/body/eval_jaxpr/reduce_sum | solution.py:163
  188.0 4.0 fusion.602
  192.0 4.0 fusion.575
  196.1 4.0 fusion.566
  200.1 4.0 fusion.557
  204.1 4.0 fusion.584
  208.1 4.0 fusion.611
  212.1 4.0 fusion.620
  216.1 7.3 %fusion.629 = (f32[16,128]{1,0:T(8,128)S(1)}, f32[16,128]{1,0:T(8,128)S(1)}, f32[16,128]{1,0:T(8,128)S(1)}, f32[16,128]{1,0:T(8,128)S(1)}, f32[16,128]{1,0:T(8,128)S(1)}, /*index=5*/f32[16,128]{1,0:T(8,128)S(1)}) fusion(f32[16,128]{1,0:T(8,128)S(1)} %bitcast.872, f32[16,128]{1,0:T(8,128)S(1)} %bitcast.736, f32[16,128]{1,0:T(8,128)S(1)} %bitcast.939, ...), kind=kLoop, calls=%fused_computation.814 | loop fusion | flops 30920704 | bytes 180256 | tf_op jit(solution)/shard_map/reduce_sum | solution.py:70
  223.4 1.7 multiply_reduce_fusion
  225.1 32.1 %all-reduce = (f32[]{:T(128)}, f32[]{:T(128)}) all-reduce(f32[]{:T(128)} %get-tuple-element.870, f32[]{:T(128)} %get-tuple-element.869), channel_id=1, replica_groups=mesh['groups'=2,'blk'=4,'oct'=2,'sub'=2] {'blk','oct','sub'}, use_global_device_ids=true, to_apply=%region_35.36 | all-reduce | flops 2 | bytes 16 | tf_op jit(solution)/shard_map/psum | solution.py:213
  258.5 0.6 fusion.632
  259.1 30.1 %psum.53 = f32[]{:T(128)} all-reduce(f32[]{:T(128)} %fusion.632), channel_id=1, replica_groups=mesh['groups'=2,'blk'=4,'oct'=2,'sub'=2] {'blk','oct','sub'}, use_global_device_ids=true, to_apply=%region_73.74 | all-reduce | flops 1 | bytes 8 | tf_op jit(solution)/shard_map/psum | solution.py:213
  290.6 29.7 %psum.54 = f32[3]{0:T(128)S(1)} all-reduce(f32[3]{0:T(128)S(1)} %get-tuple-element.918), channel_id=1, replica_groups=mesh['groups'=2,'blk'=4,'oct'=2,'sub'=2] {'blk','oct','sub'}, use_global_device_ids=true, to_apply=%region_107.108 | all-reduce | flops 3 | bytes 24 | tf_op jit(solution)/shard_map/psum | solution.py:210
  321.3 4.4 %collective-permute-start.7 = (f32[3,512]{1,0:T(4,128)S(1)}, f32[3,512]{1,0:T(4,128)S(1)}, u32[]{:S(2)}, u32[]{:S(2)}) collective-permute-start(f32[3,512]{1,0:T(4,128)S(1)} %get-tuple-element.1070), channel_id=1, source_target_pairs={{1,0},{2,1},{3,2},{4,3},{5,4},{6,5},{7,6},{8,7},{9,8},{10,9},{11,1... | collective-permute-start | bytes 18440 | tf_op jit(solution)/shard_map/ppermute | solution.py:28
  325.7 17.3 %all_gather.11 = f32[32,3,128]{2,1,0:T(4,128)S(1)} all-gather(f32[2,3,128]{2,1,0:T(4,128)S(1)} %fusion.783), channel_id=1, replica_groups=mesh['groups'=2,'blk'=4,'oct'=2,'sub'=2] {'blk','oct','sub'}, dimensions={0}, use_global_device_ids=true | all-gather | bytes 52224 | tf_op jit(solution)/shard_map/all_gather | solution.py:192
  343.0 13.0 %while.53 = (s32[]{:T(128)}, f32[2,3,128]{2,0,1:T(2,128)S(1)}, s32[2]{0:T(128)S(1)}, f32[2,16,3,128]{3,1,2,0:T(8,128)S(1)}, s32[]{:T(128)}, /*index=5*/s32[]{:T(...) while((s32[]{:T(128)}, f32[2,3,128]{2,0,1:T(2,128)S(1)}, ...), condition=%wide.region_105.106_spmd.clone.clone.clone.clone, body=%wide.region_101.105_spmd.sunk.clone.clone.clone.clone.sunk | while | flops 16765948 | bytes 2795035 | solution.py:203
  344.7 4.8 %subtract_reduce_fusion.11 = (f32[2,128]{1,0:T(2,128)S(1)}, f32[2,128]{1,0:T(2,128)S(1)}, f32[2,128]{1,0:T(2,128)S(1)}) fusion(f32[16,128]{1,0:T(8,128)S(1)} %get-tuple-element.1244, f32[128,128]{1,0:T(8,128)S(1)} %get-tuple-element.1245, pred[2,16]{1,0:T(4,128)(4,1)S(1)} %fusion.820, f32[16,128]{1,0:T(8,128)S(1)} %broadcast_add_fusion.16, ...), kind=kLoop, calls=%fused_computation.136.clone.1 | loop fusion | flops 15727872 | bytes 1282080 | tf_op jit(solution)/shard_map/while/body/eval_jaxpr/reduce_sum | solution.py:163
  351.2 4.8 %subtract_reduce_fusion.11 = (f32[2,128]{1,0:T(2,128)S(1)}, f32[2,128]{1,0:T(2,128)S(1)}, f32[2,128]{1,0:T(2,128)S(1)}) fusion(f32[16,128]{1,0:T(8,128)S(1)} %get-tuple-element.1244, f32[128,128]{1,0:T(8,128)S(1)} %get-tuple-element.1245, pred[2,16]{1,0:T(4,128)(4,1)S(1)} %fusion.820, f32[16,128]{1,0:T(8,128)S(1)} %broadcast_add_fusion.16, ...), kind=kLoop, calls=%fused_computation.136.clone.1 | loop fusion | flops 15727872 | bytes 1282080 | tf_op jit(solution)/shard_map/while/body/eval_jaxpr/reduce_sum | solution.py:163
  356.1 4.0 fusion.556
  360.1 4.0 fusion.601
  364.2 4.0 fusion.565
  368.2 4.0 fusion.574
  372.2 4.0 fusion.583
  376.2 4.0 fusion.610
  380.3 4.0 fusion.619
  384.3 7.3 %fusion.628 = (f32[16,128]{1,0:T(8,128)S(1)}, f32[16,128]{1,0:T(8,128)S(1)}, f32[16,128]{1,0:T(8,128)S(1)}, f32[16,128]{1,0:T(8,128)S(1)}, f32[16,128]{1,0:T(8,128)S(1)}, /*index=5*/f32[16,128]{1,0:T(8,128)S(1)}) fusion(f32[16,128]{1,0:T(8,128)S(1)} %bitcast.862, f32[16,128]{1,0:T(8,128)S(1)} %bitcast.737, f32[16,128]{1,0:T(8,128)S(1)} %bitcast.947, ...), kind=kLoop, calls=%fused_computation.813 | loop fusion | flops 30920704 | bytes 180256 | tf_op jit(solution)/shard_map/reduce_sum | solution.py:70
  391.5 1.6 fusion.681
  393.2 32.0 %psum.55 = f32[]{:T(128)} all-reduce(f32[]{:T(128)} %get-tuple-element.1104), channel_id=1, replica_groups=mesh['groups'=2,'blk'=4,'oct'=2,'sub'=2] {'blk','oct','sub'}, use_global_device_ids=true, to_apply=%region_109.110 | all-reduce | flops 1 | bytes 8 | tf_op jit(solution)/shard_map/psum | solution.py:222
  426.6 0.6 multiply_add_fusion.7
  427.2 0.8 multiply_subtract_fusion
  (158 shorter events, 9.6 us)
Async XLA Ops:
  0.6 45.0 %copy-start.8 = (f32[5,5,1]{1,0,2:T(8,128)S(1)}, f32[5,5,1]{1,0,2:T(8,128)}, u32[]{:S(2)}) copy-start(f32[5,5,1]{1,0,2:T(8,128)} %constant.532) | copy-start | bytes 304
  0.6 45.2 %copy-start.11 = (f32[128,5,1]{0,1,2:T(8,128)S(1)}, f32[128,5,1]{0,1,2:T(8,128)}, u32[]{:S(2)}) copy-start(f32[128,5,1]{0,1,2:T(8,128)} %constant.533) | copy-start | bytes 7684
  2.1 81.8 %collective-permute-start = (f32[5,512]{1,0:T(8,128)S(1)}, f32[5,512]{1,0:T(8,128)S(1)}, u32[]{:S(2)}, u32[]{:S(2)}) collective-permute-start(f32[5,512]{1,0:T(8,128)S(1)} %get-tuple-element.989), channel_id=1, source_target_pairs={{0,1},{1,2},{2,3},{3,4},{4,5},{5,6},{6,7},{7,8},{8,9},{9,10},{10,1... | collective-permute-start | bytes 30728 | tf_op jit(solution)/shard_map/ppermute | solution.py:26
  2.6 81.3 %collective-permute-start.2 = (f32[5,512]{1,0:T(8,128)S(1)}, f32[5,512]{1,0:T(8,128)S(1)}, u32[]{:S(2)}, u32[]{:S(2)}) collective-permute-start(f32[5,512]{1,0:T(8,128)S(1)} %get-tuple-element.990), channel_id=1, source_target_pairs={{1,0},{2,1},{3,2},{4,3},{5,4},{6,5},{7,6},{8,7},{9,8},{10,9},{11,1... | collective-permute-start | bytes 30728 | tf_op jit(solution)/shard_map/ppermute | solution.py:28
  8.6 75.2 %collective-permute-start.1 = (f32[3,512]{1,0:T(4,128)S(1)}, f32[3,512]{1,0:T(4,128)S(1)}, u32[]{:S(2)}, u32[]{:S(2)}) collective-permute-start(f32[3,512]{1,0:T(4,128)S(1)} %get-tuple-element.1085), channel_id=1, source_target_pairs={{0,1},{1,2},{2,3},{3,4},{4,5},{5,6},{6,7},{7,8},{8,9},{9,10},{10,1... | collective-permute-start | bytes 18440 | tf_op jit(solution)/shard_map/ppermute | solution.py:26
  8.6 75.2 %collective-permute-start.3 = (f32[3,512]{1,0:T(4,128)S(1)}, f32[3,512]{1,0:T(4,128)S(1)}, u32[]{:S(2)}, u32[]{:S(2)}) collective-permute-start(f32[3,512]{1,0:T(4,128)S(1)} %get-tuple-element.1086), channel_id=1, source_target_pairs={{1,0},{2,1},{3,2},{4,3},{5,4},{6,5},{7,6},{8,7},{9,8},{10,9},{11,1... | collective-permute-start | bytes 18440 | tf_op jit(solution)/shard_map/ppermute | solution.py:28
  13.1 34.7 %copy-start.10 = (f32[128,5,1]{0,1,2:T(8,128)S(1)}, f32[128,5,1]{0,1,2:T(8,128)}, u32[]{:S(2)}) copy-start(f32[128,5,1]{0,1,2:T(8,128)} %constant.534) | copy-start | bytes 7684
  47.7 1.8 copy-start.9
  51.4 18.4 %copy-start.2 = (f32[128]{0:T(128)S(1)}, f32[128]{0:T(128)}, u32[]{:S(2)}) copy-start(f32[128]{0:T(128)} %constant.2011) | copy-start | bytes 1540
  51.4 18.4 %copy-start.4 = (f32[128]{0:T(128)S(1)}, f32[128]{0:T(128)}, u32[]{:S(2)}) copy-start(f32[128]{0:T(128)} %constant.489.clone..sunk.15) | copy-start | bytes 1540
  51.4 18.4 %copy-start.5 = (f32[128]{0:T(128)S(1)}, f32[128]{0:T(128)}, u32[]{:S(2)}) copy-start(f32[128]{0:T(128)} %constant.2010) | copy-start | bytes 1540
  51.4 18.4 %copy-start.6 = (f32[128]{0:T(128)S(1)}, f32[128]{0:T(128)}, u32[]{:S(2)}) copy-start(f32[128]{0:T(128)} %constant.490.clone..sunk.15) | copy-start | bytes 1540
  51.4 18.4 %copy-start.7 = (f32[128]{0:T(128)S(1)}, f32[128]{0:T(128)}, u32[]{:S(2)}) copy-start(f32[128]{0:T(128)} %constant.2009) | copy-start | bytes 1540
  69.9 13.5 %copy-start = (s32[16,9]{1,0:T(8,128)S(1)}, s32[16,9]{1,0:T(8,128)}, u32[]{:S(2)}) copy-start(s32[16,9]{1,0:T(8,128)} %param.28) | copy-start | bytes 1732
  69.9 13.8 %copy-start.1 = (f32[2048]{0:T(1024)S(1)}, f32[2048]{0:T(1024)}, u32[]{:S(2)}) copy-start(f32[2048]{0:T(1024)} %param.25) | copy-start | bytes 24580
  69.9 14.0 %copy-start.3 = (f32[3,2048]{1,0:T(4,128)S(1)}, f32[3,2048]{1,0:T(4,128)}, u32[]{:S(2)}) copy-start(f32[3,2048]{1,0:T(4,128)} %param.24) | copy-start | bytes 73732
  153.1 34.8 %collective-permute-start.4 = (f32[3,512]{1,0:T(4,128)S(1)}, f32[3,512]{1,0:T(4,128)S(1)}, u32[]{:S(2)}, u32[]{:S(2)}) collective-permute-start(f32[3,512]{1,0:T(4,128)S(1)} %get-tuple-element.1077), channel_id=1, source_target_pairs={{0,1},{1,2},{2,3},{3,4},{4,5},{5,6},{6,7},{7,8},{8,9},{9,10},{10,1... | collective-permute-start | bytes 18440 | tf_op jit(solution)/shard_map/ppermute | solution.py:26
  153.2 34.8 %collective-permute-start.5 = (f32[3,512]{1,0:T(4,128)S(1)}, f32[3,512]{1,0:T(4,128)S(1)}, u32[]{:S(2)}, u32[]{:S(2)}) collective-permute-start(f32[3,512]{1,0:T(4,128)S(1)} %get-tuple-element.1078), channel_id=1, source_target_pairs={{1,0},{2,1},{3,2},{4,3},{5,4},{6,5},{7,6},{8,7},{9,8},{10,9},{11,1... | collective-permute-start | bytes 18440 | tf_op jit(solution)/shard_map/ppermute | solution.py:28
  321.2 34.8 %collective-permute-start.6 = (f32[3,512]{1,0:T(4,128)S(1)}, f32[3,512]{1,0:T(4,128)S(1)}, u32[]{:S(2)}, u32[]{:S(2)}) collective-permute-start(f32[3,512]{1,0:T(4,128)S(1)} %get-tuple-element.1069), channel_id=1, source_target_pairs={{0,1},{1,2},{2,3},{3,4},{4,5},{5,6},{6,7},{7,8},{8,9},{9,10},{10,1... | collective-permute-start | bytes 18440 | tf_op jit(solution)/shard_map/ppermute | solution.py:26
  321.3 34.8 %collective-permute-start.7 = (f32[3,512]{1,0:T(4,128)S(1)}, f32[3,512]{1,0:T(4,128)S(1)}, u32[]{:S(2)}, u32[]{:S(2)}) collective-permute-start(f32[3,512]{1,0:T(4,128)S(1)} %get-tuple-element.1070), channel_id=1, source_target_pairs={{1,0},{2,1},{3,2},{4,3},{5,4},{6,5},{7,6},{8,7},{9,8},{10,9},{11,1... | collective-permute-start | bytes 18440 | tf_op jit(solution)/shard_map/ppermute | solution.py:28
where the time goes:
time: 434 us; the launch traced here: 428 us
  blocking collectives  237 us (55%)
  other arithmetic  145 us (33%)
  starting transfers between devices  19 us (4%)
  matrix products  13.6 us (3%)
  between operations  5.61 us (1%)
    reduce_sum x24, other arithmetic, near_tiles(): jnp.sum(weighted * delta_x - coef_three * moments[0][:, None, :], axis=2)  106 us
    psum x3, blocking collectives, moment(): return lax.psum(jnp.sum(values, axis=1), ('blk', 'oct', 'sub'))  90.8 us
    psum x2, blocking collectives, squares(): return lax.psum(jnp.sum(resid * scaled), ('blk', 'oct', 'sub'))  62.2 us
    all_gather x3, blocking collectives, induced(): piece = lax.all_gather(weights, ('blk', 'oct', 'sub'), axis=0, tiled=True)  52.3 us
    psum x1, blocking collectives, on_device(): lax.psum(jnp.sum(direction * image), ('blk', 'oct', 'sub'))  32 us
    reduce_sum x6, other arithmetic, far_block(): field_x = jnp.sum(weighted * delta_x - coef_three * weight_x, axis=(2, 3))  28.8 us
    ppermute x4, starting transfers between devices, padded(): lax.ppermute(head, axis, [((i + 1) % count, i) for i in range(count)])  18.3 us
  transfers between devices with their start and end apart: 8, of which 0 were waited for; matrix products, arithmetic and copies ran while one was open for 11% of the time, Pallas kernels for 0%

commit v1 on v0

--- a/solution.py
+++ b/solution.py
@@ -4,6 +4,7 @@
 import numpy as np
 from jax import lax
 from jax.sharding import PartitionSpec as P
+from jax.lax import all_gather
 
 BOXES_DEV = 2
 BLOCK = 128
@@ -14,6 +15,12 @@
 layer_gap = 2.5
 thole_damp = 0.39
 highest = lax.Precision.HIGHEST
+
+
+def group_treat(sheet):
+    b_next = all_gather(sheet, ("blk", "oct", "sub"))
+    a_next = jnp.sum(b_next, 0)
+    return a_next
 
 
 def padded(cells, sides, width):
@@ -207,7 +214,7 @@
         return near + far - surface * total[:, None]
 
     def moment(values):
-        return lax.psum(jnp.sum(values, axis=1), ("blk", "oct", "sub"))
+        return group_treat(jnp.sum(values, axis=1))
 
     def squares(resid, scaled):
         return lax.psum(jnp.sum(resid * scaled), ("blk", "oct", "sub"))

time: 434 us -> 438 us (level)
    psum x3 -> x0, blocking collectives: 90.8 us -> none  [moment(): return lax.psum(jnp.sum(values, axis=1), ('blk', 'oct', 'sub'))]
    unnamed x0 -> x3, blocking collectives: none -> 90.7 us
where the time goes in v1:
time: 438 us; the launch traced here: 431 us
  blocking collectives  237 us (54%)
  other arithmetic  145 us (33%)
  starting transfers between devices  19 us (4%)
  matrix products  13.7 us (3%)
  local copies, waits for them, and re-layouts  6.48 us (1%)
  between operations  6.07 us (1%)
    reduce_sum x24, other arithmetic, near_tiles(): jnp.sum(weighted * delta_x - coef_three * moments[0][:, None, :], axis=2)  106 us
    unnamed x3, blocking collectives  90.7 us
    psum x2, blocking collectives, squares(): return lax.psum(jnp.sum(resid * scaled), ('blk', 'oct', 'sub'))  62.2 us
    all_gather x3, blocking collectives, induced(): piece = lax.all_gather(weights, ('blk', 'oct', 'sub'), axis=0, tiled=True)  52.3 us
    psum x1, blocking collectives, on_device(): lax.psum(jnp.sum(direction * image), ('blk', 'oct', 'sub'))  32 us
    reduce_sum x6, other arithmetic, far_block(): field_x = jnp.sum(weighted * delta_x - coef_three * weight_x, axis=(2, 3))  28.8 us
    ppermute x4, starting transfers between devices, padded(): lax.ppermute(head, axis, [((i + 1) % count, i) for i in range(count)])  18.3 us
  transfers between devices with their start and end apart: 8, of which 0 were waited for; matrix products, arithmetic and copies ran while one was open for 11% of the time, Pallas kernels for 0%

profile of v1, /device:TPU:0, one launch (start us, length us, event | category | flops | bytes accessed | tf_op | source)
XLA Modules:
  0.0 431.4 jit_solution(7909577379564054714)
XLA Ops:
  0.7 0.7 convert_bitcast_fusion
  1.4 0.8 pad_maximum_fusion.3
  2.6 5.0 %collective-permute-start.2 = (f32[5,512]{1,0:T(8,128)S(1)}, f32[5,512]{1,0:T(8,128)S(1)}, u32[]{:S(2)}, u32[]{:S(2)}) collective-permute-start(f32[5,512]{1,0:T(8,128)S(1)} %get-tuple-element.990), channel_id=1, source_target_pairs={{1,0},{2,1},{3,2},{4,3},{5,4},{6,5},{7,6},{8,7},{9,8},{10,9},{11,1... | collective-permute-start | bytes 30728 | tf_op jit(solution)/shard_map/ppermute | solution.py:35
  7.7 0.9 fusion.771
  8.6 4.4 %collective-permute-start.3 = (f32[3,512]{1,0:T(4,128)S(1)}, f32[3,512]{1,0:T(4,128)S(1)}, u32[]{:S(2)}, u32[]{:S(2)}) collective-permute-start(f32[3,512]{1,0:T(4,128)S(1)} %get-tuple-element.1086), channel_id=1, source_target_pairs={{1,0},{2,1},{3,2},{4,3},{5,4},{6,5},{7,6},{8,7},{9,8},{10,9},{11,1... | collective-permute-start | bytes 18440 | tf_op jit(solution)/shard_map/ppermute | solution.py:35
  13.1 0.9 fusion.777
  14.0 1.2 dynamic-slice
  16.1 29.5 %all-reduce = f32[48]{0:T(128)S(1)} all-reduce(f32[48]{0:T(128)S(1)} %dynamic-update-slice), channel_id=2, replica_groups=mesh['groups'=2,'blk'=4,'oct'=2,'sub'=2] {'blk','oct','sub'}, use_global_device_ids=true, to_apply=%add | all-reduce | flops 48 | bytes 384
  46.0 0.9 fusion.780
  47.0 0.9 fusion.778
  48.1 1.8 fusion.779
  50.0 1.8 convolution_multiply_fusion.1
  51.8 1.8 fusion.90
  54.3 17.8 %all_gather.27 = f32[32,3,128]{2,1,0:T(4,128)S(1)} all-gather(f32[2,3,128]{2,1,0:T(4,128)S(1)} %fusion.782), channel_id=1, replica_groups=mesh['groups'=2,'blk'=4,'oct'=2,'sub'=2] {'blk','oct','sub'}, dimensions={0}, use_global_device_ids=true | all-gather | bytes 52224 | tf_op jit(solution)/shard_map/all_gather | solution.py:199
  72.1 13.5 %while.51 = (s32[]{:T(128)}, f32[2,3,128]{2,0,1:T(2,128)S(1)}, s32[2]{0:T(128)S(1)}, f32[2,16,3,128]{3,1,2,0:T(8,128)S(1)}, s32[]{:T(128)}, /*index=5*/s32[]{:T(...) while((s32[]{:T(128)}, f32[2,3,128]{2,0,1:T(2,128)S(1)}, ...), condition=%wide.region_31.32_spmd.clone.clone.clone.clone, body=%wide.region_27.31_spmd.sunk.clone.clone.clone.clone.sunk | while | flops 16765948 | bytes 2795035 | solution.py:210
  72.2 0.7 dynamic_slice.84
  74.1 4.8 %subtract_reduce_fusion.9 = (f32[2,128]{1,0:T(2,128)S(1)}, f32[2,128]{1,0:T(2,128)S(1)}, f32[2,128]{1,0:T(2,128)S(1)}) fusion(f32[16,128]{1,0:T(8,128)S(1)} %get-tuple-element.1216, f32[128,128]{1,0:T(8,128)S(1)} %get-tuple-element.1217, pred[2,16]{1,0:T(4,128)(4,1)S(1)} %fusion.814, f32[16,128]{1,0:T(8,128)S(1)} %broadcast_add_fusion.12, ...), kind=kLoop, calls=%fused_computation.28.clone.1 | loop fusion | flops 15727872 | bytes 1282080 | tf_op jit(solution)/shard_map/while/body/eval_jaxpr/reduce_sum | solution.py:170
  78.9 0.7 dynamic_slice.84
  80.8 4.8 %subtract_reduce_fusion.9 = (f32[2,128]{1,0:T(2,128)S(1)}, f32[2,128]{1,0:T(2,128)S(1)}, f32[2,128]{1,0:T(2,128)S(1)}) fusion(f32[16,128]{1,0:T(8,128)S(1)} %get-tuple-element.1216, f32[128,128]{1,0:T(8,128)S(1)} %get-tuple-element.1217, pred[2,16]{1,0:T(4,128)(4,1)S(1)} %fusion.814, f32[16,128]{1,0:T(8,128)S(1)} %broadcast_add_fusion.12, ...), kind=kLoop, calls=%fused_computation.28.clone.1 | loop fusion | flops 15727872 | bytes 1282080 | tf_op jit(solution)/shard_map/while/body/eval_jaxpr/reduce_sum | solution.py:170
  86.4 4.0 fusion.558
  90.5 4.0 fusion.585
  94.5 4.0 fusion.567
  98.5 4.0 fusion.576
  102.5 4.0 fusion.603
  106.5 4.0 fusion.621
  110.5 4.0 fusion.612
  114.5 7.3 %fusion.630 = (f32[16,128]{1,0:T(8,128)S(1)}, f32[16,128]{1,0:T(8,128)S(1)}, f32[16,128]{1,0:T(8,128)S(1)}, f32[16,128]{1,0:T(8,128)S(1)}, f32[16,128]{1,0:T(8,128)S(1)}, /*index=5*/f32[16,128]{1,0:T(8,128)S(1)}) fusion(f32[16,128]{1,0:T(8,128)S(1)} %bitcast.841, f32[16,128]{1,0:T(8,128)S(1)} %bitcast.736, f32[16,128]{1,0:T(8,128)S(1)} %bitcast.932, ...), kind=kLoop, calls=%fused_computation.815 | loop fusion | flops 30920704 | bytes 180256 | tf_op jit(solution)/shard_map/reduce_sum | solution.py:77
  121.8 1.1 multiply_reduce_fusion.2
  123.2 31.6 %all-reduce.1 = f32[48]{0:T(128)S(1)} all-reduce(f32[48]{0:T(128)S(1)} %dynamic-update-slice.1), channel_id=3, replica_groups=mesh['groups'=2,'blk'=4,'oct'=2,'sub'=2] {'blk','oct','sub'}, use_global_device_ids=true, to_apply=%add.1 | all-reduce | flops 48 | bytes 384
  155.8 4.4 %collective-permute-start.5 = (f32[3,512]{1,0:T(4,128)S(1)}, f32[3,512]{1,0:T(4,128)S(1)}, u32[]{:S(2)}, u32[]{:S(2)}) collective-permute-start(f32[3,512]{1,0:T(4,128)S(1)} %get-tuple-element.1078), channel_id=1, source_target_pairs={{1,0},{2,1},{3,2},{4,3},{5,4},{6,5},{7,6},{8,7},{9,8},{10,9},{11,1... | collective-permute-start | bytes 18440 | tf_op jit(solution)/shard_map/ppermute | solution.py:35
  160.2 17.3 %all_gather.30 = f32[32,3,128]{2,1,0:T(4,128)S(1)} all-gather(f32[2,3,128]{2,1,0:T(4,128)S(1)} %fusion.684), channel_id=1, replica_groups=mesh['groups'=2,'blk'=4,'oct'=2,'sub'=2] {'blk','oct','sub'}, dimensions={0}, use_global_device_ids=true | all-gather | bytes 52224 | tf_op jit(solution)/shard_map/all_gather | solution.py:199
  177.5 13.0 %while.52 = (s32[]{:T(128)}, f32[2,3,128]{2,0,1:T(2,128)S(1)}, s32[2]{0:T(128)S(1)}, f32[2,16,3,128]{3,1,2,0:T(8,128)S(1)}, s32[]{:T(128)}, /*index=5*/s32[]{:T(...) while((s32[]{:T(128)}, f32[2,3,128]{2,0,1:T(2,128)S(1)}, ...), condition=%wide.region_67.68_spmd.clone.clone.clone.clone, body=%wide.region_63.67_spmd.sunk.clone.clone.clone.clone.sunk | while | flops 16765948 | bytes 2795035 | solution.py:210
  179.2 4.8 %subtract_reduce_fusion.10 = (f32[2,128]{1,0:T(2,128)S(1)}, f32[2,128]{1,0:T(2,128)S(1)}, f32[2,128]{1,0:T(2,128)S(1)}) fusion(f32[16,128]{1,0:T(8,128)S(1)} %get-tuple-element.1230, f32[128,128]{1,0:T(8,128)S(1)} %get-tuple-element.1231, pred[2,16]{1,0:T(4,128)(4,1)S(1)} %fusion.817, f32[16,128]{1,0:T(8,128)S(1)} %broadcast_add_fusion.14, ...), kind=kLoop, calls=%fused_computation.82.clone.1 | loop fusion | flops 15727872 | bytes 1282080 | tf_op jit(solution)/shard_map/while/body/eval_jaxpr/reduce_sum | solution.py:170
  185.7 4.8 %subtract_reduce_fusion.10 = (f32[2,128]{1,0:T(2,128)S(1)}, f32[2,128]{1,0:T(2,128)S(1)}, f32[2,128]{1,0:T(2,128)S(1)}) fusion(f32[16,128]{1,0:T(8,128)S(1)} %get-tuple-element.1230, f32[128,128]{1,0:T(8,128)S(1)} %get-tuple-element.1231, pred[2,16]{1,0:T(4,128)(4,1)S(1)} %fusion.817, f32[16,128]{1,0:T(8,128)S(1)} %broadcast_add_fusion.14, ...), kind=kLoop, calls=%fused_computation.82.clone.1 | loop fusion | flops 15727872 | bytes 1282080 | tf_op jit(solution)/shard_map/while/body/eval_jaxpr/reduce_sum | solution.py:170
  190.6 4.0 fusion.602
  194.7 4.0 fusion.575
  198.7 4.0 fusion.566
  202.7 4.0 fusion.557
  206.7 4.0 fusion.584
  210.8 4.0 fusion.611
  214.8 4.0 fusion.620
  218.8 7.3 %fusion.629 = (f32[16,128]{1,0:T(8,128)S(1)}, f32[16,128]{1,0:T(8,128)S(1)}, f32[16,128]{1,0:T(8,128)S(1)}, f32[16,128]{1,0:T(8,128)S(1)}, f32[16,128]{1,0:T(8,128)S(1)}, /*index=5*/f32[16,128]{1,0:T(8,128)S(1)}) fusion(f32[16,128]{1,0:T(8,128)S(1)} %bitcast.873, f32[16,128]{1,0:T(8,128)S(1)} %bitcast.737, f32[16,128]{1,0:T(8,128)S(1)} %bitcast.940, ...), kind=kLoop, calls=%fused_computation.814 | loop fusion | flops 30920704 | bytes 180256 | tf_op jit(solution)/shard_map/reduce_sum | solution.py:77
  226.1 1.7 multiply_reduce_fusion
  227.8 32.1 %all-reduce.3 = (f32[]{:T(128)}, f32[]{:T(128)}) all-reduce(f32[]{:T(128)} %get-tuple-element.870, f32[]{:T(128)} %get-tuple-element.869), channel_id=1, replica_groups=mesh['groups'=2,'blk'=4,'oct'=2,'sub'=2] {'blk','oct','sub'}, use_global_device_ids=true, to_apply=%region_35.36 | all-reduce | flops 2 | bytes 16 | tf_op jit(solution)/shard_map/psum | solution.py:220
  261.1 0.6 fusion.632
  261.8 30.1 %psum.30 = f32[]{:T(128)} all-reduce(f32[]{:T(128)} %fusion.632), channel_id=1, replica_groups=mesh['groups'=2,'blk'=4,'oct'=2,'sub'=2] {'blk','oct','sub'}, use_global_device_ids=true, to_apply=%region_73.74 | all-reduce | flops 1 | bytes 8 | tf_op jit(solution)/shard_map/psum | solution.py:220
  293.5 29.7 %all-reduce.2 = f32[48]{0:T(128)S(1)} all-reduce(f32[48]{0:T(128)S(1)} %dynamic-update-slice.2), channel_id=4, replica_groups=mesh['groups'=2,'blk'=4,'oct'=2,'sub'=2] {'blk','oct','sub'}, use_global_device_ids=true, to_apply=%add.2 | all-reduce | flops 48 | bytes 384
  324.2 4.4 %collective-permute-start.7 = (f32[3,512]{1,0:T(4,128)S(1)}, f32[3,512]{1,0:T(4,128)S(1)}, u32[]{:S(2)}, u32[]{:S(2)}) collective-permute-start(f32[3,512]{1,0:T(4,128)S(1)} %get-tuple-element.1070), channel_id=1, source_target_pairs={{1,0},{2,1},{3,2},{4,3},{5,4},{6,5},{7,6},{8,7},{9,8},{10,9},{11,1... | collective-permute-start | bytes 18440 | tf_op jit(solution)/shard_map/ppermute | solution.py:35
  328.6 17.3 %all_gather.33 = f32[32,3,128]{2,1,0:T(4,128)S(1)} all-gather(f32[2,3,128]{2,1,0:T(4,128)S(1)} %fusion.783), channel_id=1, replica_groups=mesh['groups'=2,'blk'=4,'oct'=2,'sub'=2] {'blk','oct','sub'}, dimensions={0}, use_global_device_ids=true | all-gather | bytes 52224 | tf_op jit(solution)/shard_map/all_gather | solution.py:199
  345.9 13.2 %while.53 = (s32[]{:T(128)}, f32[2,3,128]{2,0,1:T(2,128)S(1)}, s32[2]{0:T(128)S(1)}, f32[2,16,3,128]{3,1,2,0:T(8,128)S(1)}, s32[]{:T(128)}, /*index=5*/s32[]{:T(...) while((s32[]{:T(128)}, f32[2,3,128]{2,0,1:T(2,128)S(1)}, ...), condition=%wide.region_105.106_spmd.clone.clone.clone.clone, body=%wide.region_101.105_spmd.sunk.clone.clone.clone.clone.sunk | while | flops 16765948 | bytes 2795035 | solution.py:210
  347.7 4.8 %subtract_reduce_fusion.11 = (f32[2,128]{1,0:T(2,128)S(1)}, f32[2,128]{1,0:T(2,128)S(1)}, f32[2,128]{1,0:T(2,128)S(1)}) fusion(f32[16,128]{1,0:T(8,128)S(1)} %get-tuple-element.1244, f32[128,128]{1,0:T(8,128)S(1)} %get-tuple-element.1245, pred[2,16]{1,0:T(4,128)(4,1)S(1)} %fusion.820, f32[16,128]{1,0:T(8,128)S(1)} %broadcast_add_fusion.16, ...), kind=kLoop, calls=%fused_computation.136.clone.1 | loop fusion | flops 15727872 | bytes 1282080 | tf_op jit(solution)/shard_map/while/body/eval_jaxpr/reduce_sum | solution.py:170
  354.3 4.8 %subtract_reduce_fusion.11 = (f32[2,128]{1,0:T(2,128)S(1)}, f32[2,128]{1,0:T(2,128)S(1)}, f32[2,128]{1,0:T(2,128)S(1)}) fusion(f32[16,128]{1,0:T(8,128)S(1)} %get-tuple-element.1244, f32[128,128]{1,0:T(8,128)S(1)} %get-tuple-element.1245, pred[2,16]{1,0:T(4,128)(4,1)S(1)} %fusion.820, f32[16,128]{1,0:T(8,128)S(1)} %broadcast_add_fusion.16, ...), kind=kLoop, calls=%fused_computation.136.clone.1 | loop fusion | flops 15727872 | bytes 1282080 | tf_op jit(solution)/shard_map/while/body/eval_jaxpr/reduce_sum | solution.py:170
  359.2 4.0 fusion.556
  363.3 4.0 fusion.601
  367.3 4.0 fusion.565
  371.3 4.0 fusion.574
  375.3 4.0 fusion.583
  379.4 4.0 fusion.610
  383.4 4.0 fusion.619
  387.4 7.3 %fusion.628 = (f32[16,128]{1,0:T(8,128)S(1)}, f32[16,128]{1,0:T(8,128)S(1)}, f32[16,128]{1,0:T(8,128)S(1)}, f32[16,128]{1,0:T(8,128)S(1)}, f32[16,128]{1,0:T(8,128)S(1)}, /*index=5*/f32[16,128]{1,0:T(8,128)S(1)}) fusion(f32[16,128]{1,0:T(8,128)S(1)} %bitcast.863, f32[16,128]{1,0:T(8,128)S(1)} %bitcast.738, f32[16,128]{1,0:T(8,128)S(1)} %bitcast.948, ...), kind=kLoop, calls=%fused_computation.813 | loop fusion | flops 30920704 | bytes 180256 | tf_op jit(solution)/shard_map/reduce_sum | solution.py:77
  394.7 1.6 fusion.681
  396.4 32.0 %psum.31 = f32[]{:T(128)} all-reduce(f32[]{:T(128)} %get-tuple-element.1104), channel_id=1, replica_groups=mesh['groups'=2,'blk'=4,'oct'=2,'sub'=2] {'blk','oct','sub'}, use_global_device_ids=true, to_apply=%region_109.110 | all-reduce | flops 1 | bytes 8 | tf_op jit(solution)/shard_map/psum | solution.py:229
  429.7 0.6 multiply_add_fusion.7
  430.4 0.8 multiply_subtract_fusion
  (171 shorter events, 11.3 us)
Async XLA Ops:
  0.6 47.3 %copy-start.8 = (f32[5,5,1]{1,0,2:T(8,128)S(1)}, f32[5,5,1]{1,0,2:T(8,128)}, u32[]{:S(2)}) copy-start(f32[5,5,1]{1,0,2:T(8,128)} %constant.550) | copy-start | bytes 304
  0.6 47.5 %copy-start.11 = (f32[128,5,1]{0,1,2:T(8,128)S(1)}, f32[128,5,1]{0,1,2:T(8,128)}, u32[]{:S(2)}) copy-start(f32[128,5,1]{0,1,2:T(8,128)} %constant.551) | copy-start | bytes 7684
  2.1 84.0 %collective-permute-start = (f32[5,512]{1,0:T(8,128)S(1)}, f32[5,512]{1,0:T(8,128)S(1)}, u32[]{:S(2)}, u32[]{:S(2)}) collective-permute-start(f32[5,512]{1,0:T(8,128)S(1)} %get-tuple-element.989), channel_id=1, source_target_pairs={{0,1},{1,2},{2,3},{3,4},{4,5},{5,6},{6,7},{7,8},{8,9},{9,10},{10,1... | collective-permute-start | bytes 30728 | tf_op jit(solution)/shard_map/ppermute | solution.py:33
  2.6 83.5 %collective-permute-start.2 = (f32[5,512]{1,0:T(8,128)S(1)}, f32[5,512]{1,0:T(8,128)S(1)}, u32[]{:S(2)}, u32[]{:S(2)}) collective-permute-start(f32[5,512]{1,0:T(8,128)S(1)} %get-tuple-element.990), channel_id=1, source_target_pairs={{1,0},{2,1},{3,2},{4,3},{5,4},{6,5},{7,6},{8,7},{9,8},{10,9},{11,1... | collective-permute-start | bytes 30728 | tf_op jit(solution)/shard_map/ppermute | solution.py:35
  8.6 77.4 %collective-permute-start.1 = (f32[3,512]{1,0:T(4,128)S(1)}, f32[3,512]{1,0:T(4,128)S(1)}, u32[]{:S(2)}, u32[]{:S(2)}) collective-permute-start(f32[3,512]{1,0:T(4,128)S(1)} %get-tuple-element.1085), channel_id=1, source_target_pairs={{0,1},{1,2},{2,3},{3,4},{4,5},{5,6},{6,7},{7,8},{8,9},{9,10},{10,1... | collective-permute-start | bytes 18440 | tf_op jit(solution)/shard_map/ppermute | solution.py:33
  8.6 77.4 %collective-permute-start.3 = (f32[3,512]{1,0:T(4,128)S(1)}, f32[3,512]{1,0:T(4,128)S(1)}, u32[]{:S(2)}, u32[]{:S(2)}) collective-permute-start(f32[3,512]{1,0:T(4,128)S(1)} %get-tuple-element.1086), channel_id=1, source_target_pairs={{1,0},{2,1},{3,2},{4,3},{5,4},{6,5},{7,6},{8,7},{9,8},{10,9},{11,1... | collective-permute-start | bytes 18440 | tf_op jit(solution)/shard_map/ppermute | solution.py:35
  13.1 36.9 %copy-start.10 = (f32[128,5,1]{0,1,2:T(8,128)S(1)}, f32[128,5,1]{0,1,2:T(8,128)}, u32[]{:S(2)}) copy-start(f32[128,5,1]{0,1,2:T(8,128)} %constant.552) | copy-start | bytes 7684
  50.0 1.8 copy-start.9
  53.6 18.4 %copy-start.2 = (f32[128]{0:T(128)S(1)}, f32[128]{0:T(128)}, u32[]{:S(2)}) copy-start(f32[128]{0:T(128)} %constant.2029) | copy-start | bytes 1540
  53.6 18.4 %copy-start.4 = (f32[128]{0:T(128)S(1)}, f32[128]{0:T(128)}, u32[]{:S(2)}) copy-start(f32[128]{0:T(128)} %constant.489.clone..sunk.15) | copy-start | bytes 1540
  53.7 18.4 %copy-start.5 = (f32[128]{0:T(128)S(1)}, f32[128]{0:T(128)}, u32[]{:S(2)}) copy-start(f32[128]{0:T(128)} %constant.2028) | copy-start | bytes 1540
  53.7 18.4 %copy-start.6 = (f32[128]{0:T(128)S(1)}, f32[128]{0:T(128)}, u32[]{:S(2)}) copy-start(f32[128]{0:T(128)} %constant.490.clone..sunk.15) | copy-start | bytes 1540
  53.7 18.4 %copy-start.7 = (f32[128]{0:T(128)S(1)}, f32[128]{0:T(128)}, u32[]{:S(2)}) copy-start(f32[128]{0:T(128)} %constant.2027) | copy-start | bytes 1540
  72.1 13.5 %copy-start = (s32[16,9]{1,0:T(8,128)S(1)}, s32[16,9]{1,0:T(8,128)}, u32[]{:S(2)}) copy-start(s32[16,9]{1,0:T(8,128)} %param.28) | copy-start | bytes 1732
  72.1 13.8 %copy-start.1 = (f32[2048]{0:T(1024)S(1)}, f32[2048]{0:T(1024)}, u32[]{:S(2)}) copy-start(f32[2048]{0:T(1024)} %param.25) | copy-start | bytes 24580
  72.1 14.0 %copy-start.3 = (f32[3,2048]{1,0:T(4,128)S(1)}, f32[3,2048]{1,0:T(4,128)}, u32[]{:S(2)}) copy-start(f32[3,2048]{1,0:T(4,128)} %param.24) | copy-start | bytes 73732
  155.7 34.8 %collective-permute-start.4 = (f32[3,512]{1,0:T(4,128)S(1)}, f32[3,512]{1,0:T(4,128)S(1)}, u32[]{:S(2)}, u32[]{:S(2)}) collective-permute-start(f32[3,512]{1,0:T(4,128)S(1)} %get-tuple-element.1077), channel_id=1, source_target_pairs={{0,1},{1,2},{2,3},{3,4},{4,5},{5,6},{6,7},{7,8},{8,9},{9,10},{10,1... | collective-permute-start | bytes 18440 | tf_op jit(solution)/shard_map/ppermute | solution.py:33
  155.8 34.8 %collective-permute-start.5 = (f32[3,512]{1,0:T(4,128)S(1)}, f32[3,512]{1,0:T(4,128)S(1)}, u32[]{:S(2)}, u32[]{:S(2)}) collective-permute-start(f32[3,512]{1,0:T(4,128)S(1)} %get-tuple-element.1078), channel_id=1, source_target_pairs={{1,0},{2,1},{3,2},{4,3},{5,4},{6,5},{7,6},{8,7},{9,8},{10,9},{11,1... | collective-permute-start | bytes 18440 | tf_op jit(solution)/shard_map/ppermute | solution.py:35
  324.2 35.0 %collective-permute-start.6 = (f32[3,512]{1,0:T(4,128)S(1)}, f32[3,512]{1,0:T(4,128)S(1)}, u32[]{:S(2)}, u32[]{:S(2)}) collective-permute-start(f32[3,512]{1,0:T(4,128)S(1)} %get-tuple-element.1069), channel_id=1, source_target_pairs={{0,1},{1,2},{2,3},{3,4},{4,5},{5,6},{6,7},{7,8},{8,9},{9,10},{10,1... | collective-permute-start | bytes 18440 | tf_op jit(solution)/shard_map/ppermute | solution.py:33
  324.2 35.0 %collective-permute-start.7 = (f32[3,512]{1,0:T(4,128)S(1)}, f32[3,512]{1,0:T(4,128)S(1)}, u32[]{:S(2)}, u32[]{:S(2)}) collective-permute-start(f32[3,512]{1,0:T(4,128)S(1)} %get-tuple-element.1070), channel_id=1, source_target_pairs={{1,0},{2,1},{3,2},{4,3},{5,4},{6,5},{7,6},{8,7},{9,8},{10,9},{11,1... | collective-permute-start | bytes 18440 | tf_op jit(solution)/shard_map/ppermute | solution.py:35
